TPU v7x, 512 devices: a whole 4x8x8 slice. The times are simulated.
512 devices in a mesh: dp: 32 (over x, z), ctx: 16 (over y, core).
Axes of the slice: x: 4, y: 8, z: 8, core: 2. Of those that a mesh axis runs over, the one named last changes fastest.
Arguments:
- u_codes: bfloat16 [32, 4096, 2560], P('dp', 'ctx'), may hold values from -384 to 384
- u_scale: float32 [32, 4096, 20], P('dp', 'ctx'), may hold values from 0.0078125 to 0.03125
- w_bc: bfloat16 [2560, 256], P('ctx'), may hold values from -0.125 to 0.125
- xs: bfloat16 [32, 4096, 2560], P('dp', 'ctx'), may hold values from -6 to 6
- dt: float32 [32, 40, 4096], P('dp', None, 'ctx'), may hold values from 0.0078125 to 0.03125
- log_keep: float32 [32, 40, 4096], P('dp', None, 'ctx'), may hold values from -1.2 to 0, as said below
- dy: bfloat16 [32, 4096, 2560], P('dp', 'ctx'), may hold values from -0.0010299683 to 0.0010299683
- lengths: int32 [32, 2], P('dp'), may hold values from 0 to 4096, as said below
Outputs:
- grad_bc: float32 [2560, 256], P(('dp', 'ctx'))
- grad_dt: float32 [32, 40, 4096], P('dp', None, 'ctx')
- grad_keep: float32 [32, 40, 4096], P('dp', None, 'ctx')
Inputs may be any that keep to these rules, and one draw needn't show every extreme that they name: `lengths`: each row sums to 4096; some rows start with 0 (no document boundary inside the sequence), row 0 among them. `log_keep`: non-positive.
All inputs are finite; a program needn't handle non-finite values.
Results may differ from a plain program's by a relative error of at most 0.006.
Values may be sent and summed in bfloat16 or wider, within the bound.
A program may use at most 128 MiB of HBM per device.

v0:
```python
import jax
import jax.numpy as jnp
from jax import lax
from jax.sharding import PartitionSpec as P

D = 2560
H = 40
P_SIZE = 64
N = 128
CH = 256
QB = 128
TOK_DEV = 256


middle = lax.Precision.HIGH


def carried_in(array, axis, combine, identity, reverse):
    length, here = (lax.axis_size(axis), lax.axis_index(axis))
    everything = jax.tree.map(lambda part: lax.all_gather(part, axis), array)
    start = jax.tree.map(
        lambda part, zero: jnp.broadcast_to(jnp.asarray(zero, part.dtype), part.shape),
        array,
        identity,
    )

    def step(k, before):
        at = length - 1 - k if reverse else k
        reached = at > here if reverse else at < here
        new = combine(before, jax.tree.map(lambda part: part[at], everything))
        return jax.tree.map(lambda a, b: jnp.where(reached, a, b), new, before)

    return lax.fori_loop(0, length, step, start)


def combine(earlier, later):
    return (earlier[0] * later[0], later[0][:, None, None] * earlier[1] + later[1])


def block_setup(keep, resets):
    cumlog = jnp.cumsum(keep, axis=1)
    counts = jnp.cumsum(resets)
    final_log = cumlog[:, -1:]
    final_count = counts[-1]
    dec_start = jnp.exp(cumlog) * (counts == 0).astype(jnp.float32)[None, :]
    dec_end = jnp.exp(final_log - cumlog) * (counts == final_count).astype(jnp.float32)[None, :]
    carry = jnp.exp(final_log[:, 0]) * (final_count == 0).astype(jnp.float32)
    return (cumlog, counts, dec_start, dec_end, carry)


def intra_terms(x_rows, dy_rows, steps, cumlog, batch_c, batch_b, same, lower, cross):
    diff = cumlog[:, :, None] - cumlog[:, None, :]
    weight = jnp.where(same[None], jnp.exp(jnp.minimum(diff, 0.0)), 0.0)
    dots = jnp.einsum("thp,shp->hts", dy_rows, x_rows, preferred_element_type=jnp.float32)
    mixed = weight * dots
    scaled = (mixed * steps[:, None, :]).astype(jnp.bfloat16)
    grad_c = jnp.einsum("hts,sn->tn", scaled, batch_b, preferred_element_type=jnp.float32)
    grad_b = jnp.einsum("hts,tn->sn", scaled, batch_c, preferred_element_type=jnp.float32)
    paired = mixed * cross[None]
    grad_step = jnp.sum(paired, axis=1)
    weighted = paired * steps[:, None, :]
    before = jnp.cumsum(weighted, axis=2) - weighted
    grad_log = jnp.sum(jnp.where(lower[None], before, 0.0), axis=1)
    return (grad_c, grad_b, grad_step, grad_log)


def finish(x_full, dy_full, b_full, c_full, steps, dec_start, dec_end, carry, s_in, g_after):
    y_inter = jnp.einsum("hpn,tn->htp", s_in, c_full, precision=middle) * dec_start[:, :, None]
    x_term = jnp.einsum("thp,htp->ht", dy_full, y_inter, precision=middle)
    grad_c = jnp.einsum("ht,thp,hpn->tn", dec_start, dy_full, s_in, precision=middle)
    g_on_b = jnp.einsum("hpn,tn->htp", g_after, b_full, precision=middle)
    external = dec_end * jnp.einsum("thp,htp->ht", x_full, g_on_b, precision=middle)
    grad_b = jnp.einsum("ht,thp,hpn->tn", dec_end * steps, x_full, g_after, precision=middle)
    constant = carry * jnp.sum(g_after * s_in, axis=(1, 2))
    later = jnp.cumsum(x_term[:, ::-1], axis=1)[:, ::-1]
    z_term = steps * external
    earlier = jnp.cumsum(z_term, axis=1) - z_term
    return (grad_c, grad_b, external, later + earlier + constant[:, None])


def body(u_codes, u_scale, w_bc, xs, dt, log_keep, dy, lengths):
    u_deq = (
        (u_codes[0].astype(jnp.float32).reshape(TOK_DEV, D // QB, QB) * u_scale[0][:, :, None])
        .reshape(TOK_DEV, D)
        .astype(jnp.bfloat16)
    )
    columns = u_deq
    proj = jnp.dot(
        columns, lax.all_gather(w_bc, "ctx", axis=0, tiled=True), preferred_element_type=jnp.float32
    ).astype(jnp.bfloat16)
    offset = lax.axis_index("ctx") * TOK_DEV
    position = offset + jnp.arange(TOK_DEV, dtype=jnp.int32)
    starts = jnp.cumsum(lengths[0]) - lengths[0]
    resets = jnp.any(position[:, None] == starts[None, :], axis=1).astype(jnp.float32)
    lower = jnp.arange(CH)[:, None] >= jnp.arange(CH)[None, :]
    group = 8
    ngroup = H // group
    nblock = TOK_DEV // CH
    block = 0
    first = block * CH
    x_rows = xs[0, first : first + CH]
    dy_rows = dy[0, first : first + CH]
    batch_b = proj[first : first + CH, :N]
    batch_c = proj[first : first + CH, N:]
    step_rows = dt[0, :, first : first + CH]
    keep_rows = log_keep[0, :, first : first + CH]
    cumlog, counts, dec_start, dec_end, carry = block_setup(keep_rows, resets)
    same = lower & (counts[:, None] == counts[None, :])
    cross = jnp.dot(batch_c, batch_b.T, preferred_element_type=jnp.float32)
    x_full = x_rows.astype(jnp.float32).reshape(CH, H, P_SIZE)
    dy_full = dy_rows.astype(jnp.float32).reshape(CH, H, P_SIZE)
    b_full = batch_b.astype(jnp.float32)
    c_full = batch_c.astype(jnp.float32)
    s_local = jnp.einsum("ht,thp,tn->hpn", dec_end * step_rows, x_full, b_full, precision=middle)
    g_local = jnp.einsum("ht,thp,tn->hpn", dec_start, dy_full, c_full, precision=middle)
    forward_elems = (carry, s_local)
    reverse_elems = [(carry, g_local)]
    grouped = (
        x_rows.reshape(CH, ngroup, group, P_SIZE).transpose(1, 0, 2, 3),
        dy_rows.reshape(CH, ngroup, group, P_SIZE).transpose(1, 0, 2, 3),
        step_rows.reshape(ngroup, group, CH),
        cumlog.reshape(ngroup, group, CH),
    )

    def run_group(item, batch_c=batch_c, batch_b=batch_b, same=same, cross=cross):
        return intra_terms(item[0], item[1], item[2], item[3], batch_c, batch_b, same, lower, cross)

    inner_c, inner_b, inner_step, inner_log = lax.map(run_group, grouped)
    saved = [
        (
            x_full,
            dy_full,
            b_full,
            c_full,
            step_rows,
            dec_start,
            dec_end,
            carry,
            jnp.sum(inner_c, axis=0),
            jnp.sum(inner_b, axis=0),
            inner_step.reshape(H, CH),
            inner_log.reshape(H, CH),
        )
    ]
    identity = (jnp.ones((H,), jnp.float32), jnp.zeros((H, P_SIZE, N), jnp.float32))
    total_fwd = identity
    elem = forward_elems
    total_fwd = combine(total_fwd, elem)
    total_rev = identity
    for elem in reversed(reverse_elems):
        total_rev = combine(total_rev, elem)
    incoming = carried_in((total_fwd[0], total_fwd[1]), "ctx", combine, identity, False)
    outgoing = carried_in((total_rev[0], total_rev[1]), "ctx", combine, identity, True)
    block = 0
    state_ins = [incoming[1]]
    adjoint_afters = [None] * nblock
    suffix = outgoing
    for block in reversed(range(nblock)):
        adjoint_afters[block] = suffix[1]
        suffix = combine(suffix, reverse_elems[block])
    block = 0
    (
        x_full,
        dy_full,
        b_full,
        c_full,
        step_rows,
        dec_start,
        dec_end,
        carry,
        inner_c,
        inner_b,
        inner_step,
        inner_log,
    ) = saved[block]
    outer_c, outer_b, external, outer_log = finish(
        x_full,
        dy_full,
        b_full,
        c_full,
        step_rows,
        dec_start,
        dec_end,
        carry,
        state_ins[block],
        adjoint_afters[block],
    )
    dbc_rows = jnp.concatenate([inner_b + outer_b, inner_c + outer_c], axis=1)
    step_rows_out = inner_step + external
    log_rows_out = inner_log + outer_log
    dbc = dbc_rows.astype(jnp.bfloat16)
    grad_dt = step_rows_out[None]
    grad_keep = log_rows_out[None]
    columns = u_deq
    grad_bc = lax.psum_scatter(
        lax.dot_general(columns, dbc, (((0,), (0,)), ((), ())), preferred_element_type=jnp.float32),
        ("dp", "ctx"),
        scatter_dimension=0,
        tiled=True,
    )
    return (grad_bc, grad_dt, grad_keep)


def solution(mesh):
    placed = (
        P("dp", "ctx", None),
        P("dp", "ctx", None),
        P("ctx", None),
        P("dp", "ctx", None),
        P("dp", None, "ctx"),
        P("dp", None, "ctx"),
        P("dp", "ctx", None),
        P("dp", None),
    )
    return jax.shard_map(
        body,
        mesh=mesh,
        in_specs=placed,
        out_specs=(P(("dp", "ctx"), None), P("dp", None, "ctx"), P("dp", None, "ctx")),
        check_vma=False,
    )
```

profile of v0, /device:TPU:1, one launch (start us, length us, event | category | flops | bytes accessed | tf_op | source)
XLA Modules:
  0.0 645.5 jit_solution(8681209093092057551)
XLA Ops:
  13.0 2.5 copy.81
  16.2 2.0 fusion.18
  19.1 37.8 %all-gather.7.cloned.1.call-done = bf16[2560,256]{1,0:T(8,128)(2,1)} async-done(((bf16[160,256]{1,0:T(8,128)(2,1)}), bf16[2560,256]{1,0:T(8,128)(2,1)}) %all-gather.7.cloned.1.call-update) | async-done | bytes 1310736 | tf_op jit(solution)/shard_map/all_gather | solution.py:89
  56.9 1.9 convolution_convert_fusion
  58.8 2.0 fusion.27
  60.9 1.3 dynamic-slice
  63.1 24.3 %all-reduce = f32[640]{0:T(1024)S(1)} all-reduce(f32[640]{0:T(1024)S(1)} %dynamic-update-slice), channel_id=2, replica_groups=mesh['dp'=32,'ctx'=16] {'ctx'}, use_global_device_ids=true, to_apply=%add | all-reduce | flops 640 | bytes 5120
  87.5 1.6 copy.85
  89.8 88.0 %all-gather.9.cloned.1.call-done = f32[640,64,128]{2,1,0:T(8,128)} async-done(((f32[40,64,128]{2,1,0:T(8,128)}), f32[640,64,128]{2,1,0:T(8,128)}) %all-gather.9.cloned.1.call-update) | async-done | bytes 20971536 | tf_op jit(solution)/shard_map/all_gather | solution.py:20
  177.7 26.7 %while.48 = (s32[]{:T(128)}, f32[40,64,128]{2,1,0:T(8,128)S(1)}, s32[]{:T(128)}, f32[16,40]{1,0:T(8,128)S(1)}, f32[16,40,64,128]{3,2,1,0:T(8,128)}, /*index=5*/s32[]{:T(128)}, s32[]{:T(128)}, s32[]{:T(128)}, s32[]{:T(128)}) while((s32[]{:T(128)}, f32[40,64,128]{2,1,0:T(8,128)S(1)}, s32[]{:T(128)}, f32[16,40]{1,0:T(8,128)S(1)}, ...), condition=%wide.region_15.16_spmd.clone, body=%wide.region_14.15_spmd.clone.sunk | while | flops 1310728 | bytes 3932807 | solution.py:33
  177.7 1.6 fusion.105
  179.4 1.6 fusion.105
  181.1 1.6 fusion.105
  182.8 1.6 fusion.105
  184.4 1.6 fusion.105
  186.1 1.6 fusion.105
  187.8 1.6 fusion.105
  189.4 1.6 fusion.105
  191.1 1.6 fusion.105
  192.8 1.6 fusion.105
  194.5 1.6 fusion.105
  196.1 1.6 fusion.105
  197.8 1.6 fusion.105
  199.5 1.6 fusion.105
  201.2 1.6 fusion.105
  202.8 1.6 fusion.105
  206.7 2.0 fusion.26
  211.4 43.1 %while.47 = (s32[]{:T(128)}, f32[5,256,128]{2,1,0:T(8,128)S(1)}, f32[5,256,128]{2,1,0:T(8,128)}, f32[5,8,256]{2,1,0:T(8,128)}, f32[5,8,256]{2,1,0:T(8,128)}, /*i...) while((s32[]{:T(128)}, f32[5,256,128]{2,1,0:T(8,128)S(1)}, ...), condition=%wide.region_12.13_spmd.clone, body=%wide.region_6.12_spmd.clone.sunk | while | flops 175310848 | bytes 20909200 | solution.py:128
  212.9 2.6 multiply_reduce_fusion.4
  215.5 1.3 fusion.102
  221.5 2.7 multiply_reduce_fusion.4
  224.2 1.3 fusion.102
  230.2 2.6 multiply_reduce_fusion.4
  232.8 1.3 fusion.102
  238.8 2.6 multiply_reduce_fusion.4
  241.4 1.3 fusion.102
  247.4 2.6 multiply_reduce_fusion.4
  250.0 1.3 fusion.102
  254.5 1.1 reduce_sum.60
  257.0 1.0 copy.91
  259.6 2.6 fusion.36
  262.2 63.1 %all-gather.11.cloned.1.call-done = f32[640,64,128]{2,1,0:T(8,128)} async-done(((f32[40,64,128]{2,1,0:T(8,128)}), f32[640,64,128]{2,1,0:T(8,128)}) %all-gather.11.cloned.1.call-update) | async-done | bytes 20971536 | tf_op jit(solution)/shard_map/all_gather | solution.py:20
  325.4 26.5 %while.49 = (s32[]{:T(128)}, f32[40,64,128]{2,1,0:T(8,128)S(1)}, s32[]{:T(128)}, f32[16,40]{1,0:T(8,128)S(1)}, f32[16,40,64,128]{3,2,1,0:T(8,128)}, /*index=5*/s32[]{:T(128)}, s32[]{:T(128)}) while((s32[]{:T(128)}, f32[40,64,128]{2,1,0:T(8,128)S(1)}, s32[]{:T(128)}, f32[16,40]{1,0:T(8,128)S(1)}, f32[16,40,64,128]{3,2,1,0:T(8,128)}, ...), condition=%wide.region_18.19_spmd.clone, body=%wide.region_17.18_spmd.clone.sunk | while | flops 1310724 | bytes 3932745 | solution.py:33
  325.4 1.6 fusion.106
  327.0 1.6 fusion.106
  328.7 1.6 fusion.106
  330.4 1.6 fusion.106
  332.0 1.6 fusion.106
  333.7 1.6 fusion.106
  335.3 1.6 fusion.106
  337.0 1.6 fusion.106
  338.7 1.6 fusion.106
  340.3 1.6 fusion.106
  342.0 1.6 fusion.106
  343.6 1.6 fusion.106
  345.3 1.6 fusion.106
  346.9 1.6 fusion.106
  348.6 1.6 fusion.106
  350.3 1.6 fusion.106
  351.9 2.7 fusion.37
  354.6 2.1 fusion.38
  357.5 2.3 fusion.20
  362.0 275.7 %all-reduce.4.cloned.1.call-done = f32[2560,256]{1,0:T(8,128)} async-done(((f32[2560,256]{1,0:T(8,128)}), f32[2560,256]{1,0:T(8,128)}) %all-reduce.4.cloned.1.call-update) | async-done | bytes 2621456
  637.7 1.3 constant_dynamic-slice_fusion
  (197 shorter events, 41.6 us)
Async XLA Ops:
  7.2 49.7 %all-gather.7.cloned.1.call-start = ((), (), s32[]{:S(2)}) async-start(), calls=%async_computation | async-start | bytes 1392640 | tf_op jit(solution)/shard_map/all_gather | solution.py:89
  7.9 169.8 %all-gather.9.cloned.1.call-start = ((), (), s32[]{:S(2)}) async-start(), calls=%async_computation.1 | async-start | bytes 22282240 | tf_op jit(solution)/shard_map/all_gather | solution.py:20
  13.0 2.6 copy-start.16
  13.0 2.6 copy-start.4
  16.2 42.6 %copy-start = (bf16[1,256,2560]{1,2,0:T(8,128)(2,1)}, bf16[1,256,2560]{1,2,0:T(8,128)(2,1)S(1)}, u32[]{:S(2)}) copy-start(bf16[1,256,2560]{1,2,0:T(8,128)(2,1)S(1)} %copy.84) | copy-start | bytes 3932164
  18.3 40.5 %copy-start.2 = (bf16[256,2560]{0,1:T(8,128)(2,1)}, bf16[256,2560]{0,1:T(8,128)(2,1)S(1)}, u32[]{:S(2)}) copy-start(bf16[256,2560]{0,1:T(8,128)(2,1)S(1)} %fusion.18) | copy-start | bytes 3932164
  18.4 0.8 copy-start.10
  19.1 39.7 %copy-start.7 = (f32[256,40]{0,1:T(8,128)}, f32[256,40]{0,1:T(8,128)S(1)}, u32[]{:S(2)}) copy-start(f32[256,40]{0,1:T(8,128)S(1)} %fusion.76) | copy-start | bytes 122884
  60.8 264.5 %all-gather.11.cloned.1.call-start = ((), (), s32[]{:S(2)}) async-start(), calls=%async_computation.2 | async-start | bytes 22282240 | tf_op jit(solution)/shard_map/all_gather | solution.py:20
  89.1 117.0 %copy-start.1 = (bf16[1,256,2560]{1,2,0:T(8,128)(2,1)}, bf16[1,256,2560]{1,2,0:T(8,128)(2,1)S(1)}, u32[]{:S(2)}) copy-start(bf16[1,256,2560]{1,2,0:T(8,128)(2,1)S(1)} %copy.85) | copy-start | bytes 3932164
  204.5 0.9 copy-start.5
  206.1 0.6 copy-start.9
  208.7 428.9 %all-reduce.4.cloned.1.call-start = ((), (), s32[]{:S(2)}) async-start(), calls=%async_computation.3 | async-start | bytes 5242880
  259.6 2.6 copy-start.17
  325.4 26.5 %copy-start.8 = (f32[256,40]{0,1:T(8,128)S(1)}, f32[256,40]{0,1:T(8,128)}, u32[]{:S(2)}) copy-start(f32[256,40]{0,1:T(8,128)} %copy-done.7) | copy-start | bytes 122884
  351.9 2.7 copy-start.3
  356.7 0.8 copy-start.13
  357.5 3.6 copy-start.11
  357.5 3.8 copy-start.6
  357.5 3.8 copy-start.12
  357.5 3.8 copy-start.14
  357.5 3.8 copy-start.15
  357.5 3.8 slice-start
Sparse Core Ops, SparseCore 0:
  10.1 46.7 all-gather.6
  61.0 116.7 all-gather.8
  208.9 116.4 all-gather.10
  356.8 280.8 all-reduce.3
where the time goes:
time: 649 us; the launch traced here: 646 us
  waiting for transfers between devices  465 us (72%)
  other arithmetic  74.2 us (11%)
  matrix products  35.7 us (6%)
  local copies, waits for them, and re-layouts  28.6 us (4%)
  blocking collectives  24.3 us (4%)
  between operations  15.5 us (2%)
    unnamed x5, waiting for transfers between devices  276 us
    all_gather x2, waiting for transfers between devices, carried_in(): everything = jax.tree.map(lambda part: lax.all_gather(part, axis), array)  151 us
    select_n x32, other arithmetic, step(): return jax.tree.map(lambda a, b: jnp.where(reached, a, b), new, before)  51.8 us
    all_gather x1, waiting for transfers between devices, body(): lax.all_gather(w_bc, 'ctx', axis=0, tiled=True)  37.8 us
    unnamed x1, blocking collectives  24.3 us
    dot_general x5, matrix products, intra_terms(): jnp.einsum('thp,shp->hts', dy_rows, x_rows, preferred_element_type=jnp.fl...  13.3 us
  transfers between devices with their start and end apart: 4, of which 4 were waited for; matrix products, arithmetic and copies ran while one was open for 11% of the time, Pallas kernels for 0%

commit v1 on v0

v1 whole, which is shorter than its diff:
```python
import functools

import jax
import jax.numpy as jnp
from jax import lax
from jax.experimental import pallas as pl
from jax.experimental.pallas import tpu as pltpu
from jax.sharding import PartitionSpec as P

D = 2560
H = 40
P_SIZE = 64
N = 128
CH = 256
QB = 128
HALF = H * P_SIZE // 2
NY = 8
NX = 4
NZ = 8
ROWS_W = 160
CHUNK = 128
NCHUNK = HALF // CHUNK
SKEW = 3
SLOTS = max(NCHUNK + SKEW * (NY - 1), H // 2)
BLK = 512
F32 = jnp.float32
BF16 = jnp.bfloat16
MESH = pl.DeviceIdType.MESH
EXACT = lax.Precision.HIGHEST
NT = (((1,), (1,)), ((), ()))
TN = (((0,), (0,)), ((), ()))


def dot(a, b, dims=None, precision=None):
    if dims is None:
        dims = (((1,), (0,)), ((), ()))
    return lax.dot_general(a, b, dims, precision=precision, preferred_element_type=F32)


def split(v):
    hi = v.astype(BF16)
    return hi, (v - hi.astype(F32)).astype(BF16)


def dot2(pair, b, dims=None):
    return dot(pair[0], b, dims) + dot(pair[1], b, dims)


def where_am_i():
    dp = lax.axis_index("dp")
    ctx = lax.axis_index("ctx")
    return dp, ctx, lax.div(ctx, 2), lax.rem(ctx, 2)


def rcopy(src, dst, send, recv, dev):
    return pltpu.make_async_remote_copy(
        src_ref=src, dst_ref=dst, send_sem=send, recv_sem=recv, device_id=dev, device_id_type=MESH
    )


def greet(peers):
    barrier = pltpu.get_barrier_semaphore()
    for dev in peers:
        pl.semaphore_signal(barrier, inc=1, device_id=dev, device_id_type=MESH)
    return barrier, len(peers)


def project_kernel(codes_ref, scale_ref, w_ref, u_ref, proj_ref, w_all, s1, r1, s2, r2, lsem):
    dp, ctx, y, c = where_am_i()
    partner = (dp, 2 * y + 1 - c)
    ydev = [(dp, lax.rem(y + d, NY) * 2 + c) for d in range(NY)]
    barrier, count = greet([partner] + ydev[1:])
    pl.semaphore_wait(barrier, count)

    def rows(i):
        return pl.ds(pl.multiple_of(i * ROWS_W, 32), ROWS_W)

    order = (4, 3, 5, 2, 6, 1, 7)
    sends = {}
    for d in order:
        sends[d] = rcopy(w_ref, w_all.at[rows(ctx)], s1.at[d], r1.at[d], ydev[d])
        sends[d].start()
    relay = {0: rcopy(w_ref, w_all.at[rows(ctx)], s2.at[0], r2.at[0], partner)}
    relay[0].start()
    local = pltpu.make_async_copy(w_ref, w_all.at[rows(ctx)], lsem)
    local.start()
    for j in range(D // QB):
        at = slice(j * QB, (j + 1) * QB)
        u_ref[:, at] = (codes_ref[:, at].astype(F32) * scale_ref[:, j : j + 1]).astype(BF16)
    local.wait()
    for d in (1, 7, 2, 6, 3, 5, 4):
        sends[d].wait_recv()
        got = rows(lax.rem(y + NY - d, NY) * 2 + c)
        relay[d] = rcopy(w_all.at[got], w_all.at[got], s2.at[d], r2.at[d], partner)
        relay[d].start()
    for d in range(NY):
        relay[d].wait_recv()
    proj_ref[...] = dot(u_ref[...], w_all[...]).astype(BF16)
    for d in order:
        sends[d].wait_send()
    for d in range(NY):
        relay[d].wait_send()


def mixer_kernel(
    marks, x_ref, dy_ref, proj_ref, dt_ref, keep_ref, gdt_ref, gkeep_ref, dbc_ref,
    dyw, xw, sloc, gloc, prt_s, prt_g, c_own, c_prt,
    fsend, frecv, vsend, vrecv, s_all, g_all, os, og,
    racc, cacc, ssum, bound, cross, cumr, cum_t, ds_t, de_t, dt_t,
    ps, pr, fs, fr, vs, vr, oss, osr, ogs, ogr,
):
    dp, ctx, y, c = where_am_i()
    partner = (dp, 2 * y + 1 - c)
    ahead = (dp, lax.rem(y + 1, NY) * 2 + c)
    behind = (dp, lax.rem(y + NY - 1, NY) * 2 + c)
    barrier, count = greet([partner, ahead, behind])
    r_eff, r_end, limit = marks[0], marks[1], marks[2]

    def iota(shape, dim):
        return lax.broadcasted_iota(jnp.int32, shape, dim)

    row, col = iota((CH, CH), 0), iota((CH, CH), 1)
    same = jnp.where(row >= r_eff, 1, 0) == jnp.where(col >= r_eff, 1, 0)
    bound[...] = jnp.where((col <= row) & same, 0.0, -1e30)
    upto = jnp.where(row <= col, 1.0, 0.0)
    eye = jnp.where(row == col, 1.0, 0.0)
    pad = jnp.zeros((128 - H, CH), F32)
    keep_p = jnp.concatenate([keep_ref[...], pad], axis=0)
    cum_p = dot(keep_p, upto, precision=EXACT)
    cumr[...] = cum_p[:H]
    cum = jnp.transpose(cum_p)
    cum_t[...] = cum
    dts = jnp.transpose(jnp.concatenate([dt_ref[...], pad], axis=0))
    tcol = iota((CH, 128), 0)
    ds = jnp.where(tcol < limit, jnp.exp(cum), 0.0)
    de = jnp.where(tcol >= r_end, jnp.exp(cum[CH - 1 : CH, :] - cum), 0.0)
    ds_t[...] = ds
    de_t[...] = de
    dt_t[...] = dts
    carry = jnp.where(CH - 1 < limit, jnp.exp(cum_p[:H, CH - 1 : CH]), 0.0)
    c_own[...] = jnp.broadcast_to(carry, (H, 128))

    def halves(v):
        return jnp.concatenate(split(v), axis=1)

    ds_hl, ws_hl = halves(ds), halves(de * dts)
    b_mat, c_mat = proj_ref[:, :N], proj_ref[:, N:]

    def local_states(g, _):
        at = pl.ds(pl.multiple_of(g * BLK, BLK), BLK)
        head = lax.rem(iota((CH, BLK), 0), 128)
        spread = jnp.where(head == 8 * g + lax.div(iota((CH, BLK), 1), P_SIZE), 1.0, 0.0).astype(BF16)
        dyb = split(dy_ref[:, at].astype(F32) * dot(ds_hl, spread))
        xb = split(x_ref[:, at].astype(F32) * dot(ws_hl, spread))
        for n in range(2):
            dyw[n, :, at] = dyb[n]
            xw[n, :, at] = xb[n]
        sloc[at, :] = dot2(xb, b_mat, TN)
        gloc[at, :] = dot2(dyb, c_mat, TN)
        return 0

    lax.fori_loop(0, H * P_SIZE // BLK, local_states, 0)
    pl.semaphore_wait(barrier, count)
    mine = pl.multiple_of(c * HALF, 128)
    theirs = pl.ds(pl.multiple_of((1 - c) * HALF, 128), HALF)
    swap = [
        rcopy(c_own, c_prt, ps.at[0], pr.at[0], partner),
        rcopy(sloc.at[theirs], prt_s, ps.at[1], pr.at[1], partner),
        rcopy(gloc.at[theirs], prt_g, ps.at[2], pr.at[2], partner),
    ]
    for one in swap:
        one.start()

    cross[...] = dot(c_mat, b_mat, NT)
    ssum[...] = jnp.zeros_like(ssum)
    racc[...] = jnp.zeros_like(racc)

    @pl.when(y == 0)
    def _():
        frecv[...] = jnp.zeros_like(frecv)

    @pl.when(y == NY - 1)
    def _():
        vrecv[...] = jnp.zeros_like(vrecv)

    lane = iota((CH, 128), 1)
    first = c == 0

    def chunk_rows(i):
        return pl.ds(pl.multiple_of(i * CHUNK, CHUNK), CHUNK)

    def decay(ref, i):
        h = c * (H // 2) + 2 * i
        return jnp.concatenate(
            [jnp.broadcast_to(ref[pl.ds(h + j, 1), :], (P_SIZE, N)) for j in range(2)], axis=0
        )

    def pick(i, own, other):
        a = own[pl.ds(pl.multiple_of(mine + i * CHUNK, CHUNK), CHUNK), :]
        b = other[chunk_rows(i), :]
        return jnp.where(first, a, b), jnp.where(first, b, a)

    def f_copy(i):
        return rcopy(fsend.at[chunk_rows(i)], frecv.at[chunk_rows(i)], fs.at[i], fr.at[i], ahead)

    def v_copy(i):
        return rcopy(vsend.at[chunk_rows(i)], vrecv.at[chunk_rows(i)], vs.at[i], vr.at[i], behind)

    def full_rows(i):
        return pl.ds(pl.multiple_of(mine + i * CHUNK, CHUNK), CHUNK)

    def s_copy(i):
        return rcopy(os.at[chunk_rows(i)], s_all.at[full_rows(i)], oss.at[i], osr.at[i], partner)

    def g_copy(i):
        return rcopy(og.at[chunk_rows(i)], g_all.at[full_rows(i)], ogs.at[i], ogr.at[i], partner)

    def slot(k, _):
        @pl.when(k < H // 2)
        def _():
            at = pl.ds(pl.multiple_of(k * 128, 128), 128)
            x2, dy2 = x_ref[:, at], dy_ref[:, at]
            turned = pltpu.roll(cum_t[...], lax.rem(128 - 2 * k, 128), 1)
            for j in range(2):
                h = 2 * k + j
                xm = jnp.where((lane < P_SIZE) if j == 0 else (lane >= P_SIZE), x2, jnp.zeros_like(x2))
                dots = dot(dy2, xm, NT)
                diff = turned[:, j : j + 1] - cumr[pl.ds(h, 1), :]
                mixed = jnp.exp(jnp.minimum(diff, bound[...])) * dots
                pair = mixed * cross[...]
                steps = dt_ref[pl.ds(h, 1), :]
                ssum[...] += mixed * steps
                cacc[pl.ds(h, 1), :] = jnp.sum(pair, axis=0, keepdims=True)
                rsum = jnp.sum(pair * steps, axis=1, keepdims=True)
                racc[...] += jnp.where(lane == h, rsum, 0.0)

        @pl.when(k == 0)
        def _():
            for one in swap:
                one.wait_recv()

        i = k - SKEW * y

        @pl.when((i >= 0) & (i < NCHUNK))
        def _():
            @pl.when(y > 0)
            def _():
                f_copy(i).wait_recv()

            a0, a1 = decay(c_own, i), decay(c_prt, i)
            a0, a1 = jnp.where(first, a0, a1), jnp.where(first, a1, a0)
            s0, s1 = pick(i, sloc, prt_s)
            state = frecv[chunk_rows(i), :].astype(F32)
            mid = a0 * state + s0

            @pl.when(y < NY - 1)
            def _():
                fsend[chunk_rows(i), :] = (a1 * mid + s1).astype(BF16)
                f_copy(i).start()

            os[chunk_rows(i), :] = jnp.where(first, mid, state)
            s_copy(i).start()
            s_all[full_rows(i), :] = jnp.where(first, state, mid)

        q = k - SKEW * (NY - 1 - y)

        @pl.when((q >= 0) & (q < NCHUNK))
        def _():
            @pl.when(y < NY - 1)
            def _():
                v_copy(q).wait_recv()

            a0, a1 = decay(c_own, q), decay(c_prt, q)
            a0, a1 = jnp.where(first, a0, a1), jnp.where(first, a1, a0)
            g0, g1 = pick(q, gloc, prt_g)
            state = vrecv[chunk_rows(q), :].astype(F32)
            mid = a1 * state + g1

            @pl.when(y > 0)
            def _():
                vsend[chunk_rows(q), :] = (a0 * mid + g0).astype(BF16)
                v_copy(q).start()

            og[chunk_rows(q), :] = jnp.where(first, state, mid)
            g_copy(q).start()
            g_all[full_rows(q), :] = jnp.where(first, mid, state)

        return 0

    lax.fori_loop(0, SLOTS, slot, 0)

    def drain(i, _):
        s_copy(i).wait()
        g_copy(i).wait()

        @pl.when(y < NY - 1)
        def _():
            f_copy(i).wait_send()

        @pl.when(y > 0)
        def _():
            v_copy(i).wait_send()

        return 0

    lax.fori_loop(0, NCHUNK, drain, 0)
    for one in swap:
        one.wait_send()

    def outer(g, sums):
        x_t, e_t, gc, gb_, const = sums
        at = pl.ds(pl.multiple_of(g * BLK, BLK), BLK)
        s_blk, g_blk = s_all[at, :], g_all[at, :]
        gather = jnp.where(8 * g + lax.div(iota((BLK, 128), 0), P_SIZE) == iota((BLK, 128), 1), 1.0, 0.0).astype(BF16)
        fold = jnp.where(8 * g + lax.div(iota((128, BLK), 1), P_SIZE) == iota((128, BLK), 0), 1.0, 0.0).astype(BF16)
        both = split(s_blk * g_blk)
        s_blk, g_blk = split(s_blk), split(g_blk)
        inner_y = dot(c_mat, s_blk[0], NT) + dot(c_mat, s_blk[1], NT)
        inner_x = dot(b_mat, g_blk[0], NT) + dot(b_mat, g_blk[1], NT)
        prod_y = split(dy_ref[:, at].astype(F32) * inner_y)
        prod_x = split(x_ref[:, at].astype(F32) * inner_x)
        return (
            x_t + dot2(prod_y, gather),
            e_t + dot2(prod_x, gather),
            gc + dot2((dyw[0, :, at], dyw[1, :, at]), s_blk[0]) + dot(dyw[0, :, at], s_blk[1]),
            gb_ + dot2((xw[0, :, at], xw[1, :, at]), g_blk[0]) + dot(xw[0, :, at], g_blk[1]),
            const + dot(fold, both[0]) + dot(fold, both[1]),
        )

    sums = split(ssum[...])
    zero = jnp.zeros((CH, 128), F32)
    start = (zero, zero, dot2(sums, b_mat), dot2(sums, c_mat, TN), jnp.zeros((128, 128), F32))
    x_t, e_t, gc, gb_, const = lax.fori_loop(0, H * P_SIZE // BLK, outer, start)
    dbc_ref[:, :N] = gb_.astype(BF16)
    dbc_ref[:, N:] = gc.astype(BF16)
    ext_t = e_t * de_t[...]
    ext = jnp.transpose(ext_t)[:H]
    z = jnp.transpose(ext_t * dt_t[...])[:H]
    late = jnp.transpose(x_t * ds_t[...] + racc[...])[:H]
    gdt_ref[...] = cacc[...] + ext
    since = jnp.where(row >= col, 1.0, 0.0)
    before = jnp.where(row < col, 1.0, 0.0)
    total = jnp.sum(const, axis=1, keepdims=True)[:H] * c_own[:, :1]
    gkeep_ref[...] = (
        dot(late - cacc[...] * dt_ref[...], since, precision=EXACT) + dot(z, before, precision=EXACT) + total
    )


def reduce_kernel(
    u_ref, dbc_ref, out_ref, own, psend, precv, xsend, xrecv, zsum, zsend, zrecv, tsend, trecv,
    ps, pr, xs_, xr, zs, zr, ts, tr,
):
    dp, ctx, y, c = where_am_i()
    x, z = lax.div(dp, NZ), lax.rem(dp, NZ)
    partner = (dp, 2 * y + 1 - c)
    xdev = [(lax.rem(x + d, NX) * NZ + z, ctx) for d in range(NX)]
    zdev = [(x * NZ + lax.rem(z + d, NZ), ctx) for d in range(NZ)]
    tdev = [(dp, lax.rem(ctx + d, 2 * NY)) for d in range(2 * NY)]
    barrier, count = greet(xdev[1:] + zdev[1:] + tdev[1:])
    first = c == 0
    d_b, d_c = dbc_ref[:, :N], dbc_ref[:, N:]
    d_own = jnp.where(first, d_b, d_c)
    d_oth = jnp.where(first, d_c, d_b)
    span = D // NX
    piece = span // NZ
    order = (2, 1, 3, 0)

    def cols(d):
        return pl.ds(pl.multiple_of(lax.rem(x + d, NX) * span, 128), span)

    pc = {}
    for n, d in enumerate(order):
        psend[d] = dot(u_ref[:, cols(d)], d_oth, TN)
        if n == 0:
            pl.semaphore_wait(barrier, count)
        pc[d] = rcopy(psend.at[d], precv.at[d], ps.at[d], pr.at[d], partner)
        pc[d].start()
    xc = {}
    for d in order:
        part = dot(u_ref[:, cols(d)], d_own, TN)
        pc[d].wait_recv()
        if d == 0:
            own[...] = part + precv[0]
        else:
            xsend[d] = (part + precv[d]).astype(BF16)
            xc[d] = rcopy(xsend.at[d], xrecv.at[d], xs_.at[d], xr.at[d], xdev[d])
            xc[d].start()
    for d in (1, 3, 2):
        xc[d].wait_recv()
    zsum[...] = own[...] + xrecv[1].astype(F32) + xrecv[2].astype(F32) + xrecv[3].astype(F32)
    zc = {}
    for d in (4, 3, 5, 2, 6, 1, 7):
        at = pl.ds(pl.multiple_of(lax.rem(z + d, NZ) * piece, 16), piece)
        zsend[d] = zsum[at, :].astype(BF16)
        zc[d] = rcopy(zsend.at[d], zrecv.at[d], zs.at[d], zr.at[d], zdev[d])
        zc[d].start()
    total = zsum[pl.ds(pl.multiple_of(z * piece, 16), piece), :]
    for d in (1, 7, 2, 6, 3, 5, 4):
        zc[d].wait_recv()
        total = total + zrecv[d].astype(F32)
    tsend[...] = jnp.zeros_like(tsend)
    for i in range(2 * NY):
        tsend[i, 0:5, :] = total[5 * i : 5 * i + 5, :]
    tc = {}
    for d in range(1, 2 * NY):
        tc[d] = rcopy(
            tsend.at[lax.rem(ctx + d, 2 * NY)], trecv.at[d], ts.at[d], tr.at[d], tdev[d]
        )
        tc[d].start()
    same = tsend[ctx]
    other = jnp.zeros((8, N), F32)
    for d in range(1, 2 * NY):
        tc[d].wait_recv()
        if d % 2 == 0:
            same = same + trecv[d]
        else:
            other = other + trecv[d]
    out_ref[:, :N] = jnp.where(first, same, other)[:5]
    out_ref[:, N:] = jnp.where(first, other, same)[:5]
    for group in (pc, xc, zc, tc):
        for one in group.values():
            one.wait_send()


VMEM = pl.BlockSpec(memory_space=pltpu.VMEM)
DMA = pltpu.SemaphoreType.DMA


def params(i):
    return pltpu.CompilerParams(collective_id=i, has_side_effects=True, vmem_limit_bytes=60 * 1024 * 1024)


def body(u_codes, u_scale, w_bc, xs, dt, log_keep, dy, lengths):
    v = pltpu.VMEM
    u, proj = pl.pallas_call(
        project_kernel,
        out_shape=(jax.ShapeDtypeStruct((CH, D), BF16), jax.ShapeDtypeStruct((CH, 2 * N), BF16)),
        in_specs=[VMEM] * 3,
        out_specs=(VMEM, VMEM),
        scratch_shapes=[v((D, 2 * N), BF16), DMA((NY,)), DMA((NY,)), DMA((NY,)), DMA((NY,)), DMA],
        compiler_params=params(0),
        name="project",
    )(u_codes[0], u_scale[0], w_bc)
    offset = lax.axis_index("ctx") * CH
    at = lengths[0, 0] - offset
    r_eff = jnp.where(at < 0, 1 << 20, at)
    r_end = jnp.where(r_eff < CH, r_eff, 0)
    limit = jnp.where(offset > 0, r_eff, 0)
    marks = jnp.stack([r_eff, r_end, limit]).astype(jnp.int32)
    hp = H * P_SIZE
    gdt, gkeep, dbc = pl.pallas_call(
        mixer_kernel,
        out_shape=(
            jax.ShapeDtypeStruct((H, CH), F32),
            jax.ShapeDtypeStruct((H, CH), F32),
            jax.ShapeDtypeStruct((CH, 2 * N), BF16),
        ),
        in_specs=[pl.BlockSpec(memory_space=pltpu.SMEM)] + [VMEM] * 5,
        out_specs=(VMEM,) * 3,
        scratch_shapes=[
            v((2, CH, hp), BF16), v((2, CH, hp), BF16), v((hp, N), F32), v((hp, N), F32),
            v((HALF, N), F32), v((HALF, N), F32),
            v((H, 128), F32), v((H, 128), F32),
            v((HALF, N), BF16), v((HALF, N), BF16), v((HALF, N), BF16), v((HALF, N), BF16),
            v((hp, N), F32), v((hp, N), F32), v((HALF, N), F32), v((HALF, N), F32),
            v((CH, 128), F32), v((H, CH), F32), v((CH, CH), F32), v((CH, CH), F32), v((CH, CH), F32),
            v((H, CH), F32), v((CH, 128), F32), v((CH, 128), F32), v((CH, 128), F32), v((CH, 128), F32),
            DMA((3,)), DMA((3,)),
        ] + [DMA((NCHUNK,))] * 8,
        compiler_params=params(1),
        name="mixer",
    )(marks, xs[0], dy[0], proj, dt[0], log_keep[0])
    span = D // NX
    grad = pl.pallas_call(
        reduce_kernel,
        out_shape=jax.ShapeDtypeStruct((5, 2 * N), F32),
        in_specs=[VMEM] * 2,
        out_specs=VMEM,
        scratch_shapes=[
            v((span, N), F32), v((NX, span, N), F32), v((NX, span, N), F32),
            v((NX, span, N), BF16), v((NX, span, N), BF16), v((span, N), F32),
            v((NZ, span // NZ, N), BF16), v((NZ, span // NZ, N), BF16),
            v((2 * NY, 8, N), F32), v((2 * NY, 8, N), F32),
            DMA((NX,)), DMA((NX,)), DMA((NX,)), DMA((NX,)), DMA((NZ,)), DMA((NZ,)),
            DMA((2 * NY,)), DMA((2 * NY,)),
        ],
        compiler_params=params(2),
        name="reduce",
    )(u, dbc)
    return grad, gdt[None], gkeep[None]


def solution(mesh):
    placed = (
        P("dp", "ctx", None),
        P("dp", "ctx", None),
        P("ctx", None),
        P("dp", "ctx", None),
        P("dp", None, "ctx"),
        P("dp", None, "ctx"),
        P("dp", "ctx", None),
        P("dp", None),
    )
    return jax.shard_map(
        body,
        mesh=mesh,
        in_specs=placed,
        out_specs=(P(("dp", "ctx"), None), P("dp", None, "ctx"), P("dp", None, "ctx")),
        check_vma=False,
    )
```

time: 649 us -> 123 us (0.19)
  waiting for transfers between devices: 465 us -> 0 us
  Pallas kernels: 0 us -> 117 us
  other arithmetic: 74.2 us -> 0.65 us
  matrix products: 35.7 us -> 0 us
  local copies, waits for them, and re-layouts: 28.6 us -> 4.02 us
  blocking collectives: 24.3 us -> 0 us
  between operations: 15.5 us -> 1.33 us
    unnamed x5 -> x0, waiting for transfers between devices: 276 us -> none
    all_gather x3 -> x0, waiting for transfers between devices: 189 us -> none  [the longest x2 151 us: carried_in(): everything = jax.tree.map(lambda part: lax.all_gather(part, axis), array)]
    pallas_call x0 -> x3, Pallas kernels: none -> 117 us  [the longest x1 51.7 us: body(): pl.pallas_call(mixer_kernel, out_shape=(jax.ShapeDtypeStruct((H, CH), F32...]
    select_n x32 -> x0, other arithmetic: 51.8 us -> none  [step(): return jax.tree.map(lambda a, b: jnp.where(reached, a, b), new, before)]
    dot_general x24 -> x0, matrix products: 35.7 us -> none  [the longest x5 13.3 us: intra_terms(): jnp.einsum('thp,shp->hts', dy_rows, x_rows, preferred_element_type=jnp.fl...]
    unnamed x1 -> x0, blocking collectives: 24.3 us -> none
    another operation x31 -> x1, other arithmetic: 11.2 us -> 0.65 us  [body(): marks = jnp.stack([r_eff, r_end, limit]).astype(jnp.int32)]
  transfers between devices with their start and end apart: 4 -> 0, of which waited for: 4 -> 0; matrix products, arithmetic and copies ran while one was open for 11% -> 0% of each run, Pallas kernels for 0% -> 0%
where the time goes in v1:
time: 123 us
  Pallas kernels  117 us (95%)
  local copies, waits for them, and re-layouts  4.02 us (3%)
  between operations  1.33 us (1%)
    pallas_call x1, Pallas kernels, body(): pl.pallas_call(mixer_kernel, out_shape=(jax.ShapeDtypeStruct((H, CH), F32...  51.7 us
    pallas_call x1, Pallas kernels, body(): pl.pallas_call(reduce_kernel, out_shape=jax.ShapeDtypeStruct((5, 2 * N),...  37.4 us
    pallas_call x1, Pallas kernels, body(): pl.pallas_call(project_kernel, out_shape=(jax.ShapeDtypeStruct((CH, D), B...  27.9 us
    unnamed x8, local copies, waits for them, and re-layouts  4.02 us

profile of v1, /device:TPU:1, one launch (start us, length us, event | category | flops | bytes accessed | tf_op | source)
XLA Modules:
  0.0 123.1 jit_solution(9659904283703116340)
XLA Ops:
  1.3 0.7 pad_add_fusion.marks
  1.9 1.5 %copy.11 = f32[1,256,20]{2,1,0:T(8,128)} copy(f32[1,256,20]{1,0,2:T(1,128)} %param.9) | data formatting | bytes 40960 | tf_op args[1]
  3.4 27.9 %project.1 = (bf16[256,2560]{1,0:T(8,128)(2,1)}, bf16[256,256]{1,0:T(8,128)(2,1)}) custom-call(bf16[256,2560]{1,0:T(8,128)(2,1)} %bitcast.13, f32[256,20]{1,0:T(8,128)} %bitcast.16, bf16[160,256]{1,0:T(8,128)(2,1)} %w_ref.1), custom_call_target="tpu_custom_call" | custom-call | tf_op jit(solution)/shard_map/project/pallas_call | solution.py:435
  31.3 51.7 %mixer.1 = (f32[40,256]{1,0:T(8,128)}, f32[40,256]{1,0:T(8,128)}, bf16[256,256]{1,0:T(8,128)(2,1)}) custom-call(s32[3]{0:T(128)} %pad_add_fusion.marks, bf16[256,2560]{1,0:T(8,128)(2,1)} %bitcast.14, bf16[256,2560]{1,0:T(8,128)(2,1)} %bitcast.15, bf16[256,256]{1,0:T(8,128)(2,1)} %get-tuple-element.9.proj_ref, f32[40,256]{1,0:T(8,128)} %bitcast.19, ...), custom_call_target="tpu_custom_call" | custom-call | tf_op jit(solution)/shard_map/mixer/pallas_call | solution.py:451
  83.1 0.0 copy-start.1
  83.1 0.0 copy-start
  83.1 37.4 %reduce.1 = f32[5,256]{1,0:T(8,128)} custom-call(bf16[256,2560]{1,0:T(8,128)(2,1)} %get-tuple-element.8.u_ref, bf16[256,256]{1,0:T(8,128)(2,1)} %get-tuple-element.10.dbc_ref), custom_call_target="tpu_custom_call" | custom-call | tf_op jit(solution)/shard_map/reduce/pallas_call | solution.py:474
  120.5 1.3 %copy.15 = f32[5,256]{1,0:T(8,128)} copy(f32[5,256]{1,0:T(8,128)} %reduce.1) | data formatting | bytes 10240
  121.8 0.0 copy-done.1
  121.8 0.6 copy.16
  122.4 0.0 copy-done
  122.4 0.6 copy.17
Async XLA Ops:
  83.1 38.8 %copy-start.1 = (f32[40,256]{1,0:T(8,128)S(1)}, f32[40,256]{1,0:T(8,128)}, u32[]{:S(2)}) copy-start(f32[40,256]{1,0:T(8,128)} %get-tuple-element.11) | copy-start | bytes 122884
  83.1 39.4 %copy-start = (f32[40,256]{1,0:T(8,128)S(1)}, f32[40,256]{1,0:T(8,128)}, u32[]{:S(2)}) copy-start(f32[40,256]{1,0:T(8,128)} %get-tuple-element.12) | copy-start | bytes 122884

commit v2 on v1

v2 whole, which is shorter than its diff:
```python
import functools

import jax
import jax.numpy as jnp
from jax import lax
from jax.experimental import pallas as pl
from jax.experimental.pallas import tpu as pltpu
from jax.sharding import PartitionSpec as P

D = 2560
H = 40
P_SIZE = 64
N = 128
CH = 256
QB = 128
HALF = H * P_SIZE // 2
NY = 8
NX = 4
NZ = 8
ROWS_W = 160
CHUNK = 128
NCHUNK = HALF // CHUNK
SKEW = 4
SLOTS = max(NCHUNK + SKEW * (NY - 1), H // 2)
BLK = 512
F32 = jnp.float32
BF16 = jnp.bfloat16
MESH = pl.DeviceIdType.MESH
EXACT = lax.Precision.HIGHEST
NT = (((1,), (1,)), ((), ()))
TN = (((0,), (0,)), ((), ()))


def dot(a, b, dims=None, precision=None):
    if dims is None:
        dims = (((1,), (0,)), ((), ()))
    return lax.dot_general(a, b, dims, precision=precision, preferred_element_type=F32)


def split(v):
    hi = v.astype(BF16)
    return hi, (v - hi.astype(F32)).astype(BF16)


def dot2(pair, b, dims=None):
    return dot(pair[0], b, dims) + dot(pair[1], b, dims)


def where_am_i():
    dp = lax.axis_index("dp")
    ctx = lax.axis_index("ctx")
    return dp, ctx, lax.div(ctx, 2), lax.rem(ctx, 2)


def rcopy(src, dst, send, recv, dev):
    return pltpu.make_async_remote_copy(
        src_ref=src, dst_ref=dst, send_sem=send, recv_sem=recv, device_id=dev, device_id_type=MESH
    )


def iota(shape, dim):
    return lax.broadcasted_iota(jnp.int32, shape, dim)


def greet(peers):
    barrier = pltpu.get_barrier_semaphore()
    for dev in peers:
        pl.semaphore_signal(barrier, inc=1, device_id=dev, device_id_type=MESH)
    return barrier, len(peers)


def mixer_kernel(
    marks, codes_ref, scale_ref, w_ref, x_ref, dy_ref, dt_ref, keep_ref, grad_ref, gdt_ref, gkeep_ref,
    u_t, w_all, u_ref,
    dyw, xw, sloc, gloc, prt_s, prt_g, c_own, c_prt,
    fsend, frecv, vsend, vrecv, s_all, g_all, os, og,
    racc, cacc, ssum, bound, cross, cumr, cum_t, ds_t, de_t, dt_t,
    own, psend, precv, xsend, xrecv, zsum, zsend, zrecv, tsend, trecv,
    ws, wr, rs, rr, lsem,
    ps, pr, fs, fr, vs, vr, oss, osr, ogs, ogr,
    qs, qr, xs_, xr, zs, zr, ts, tr,
):
    dp, ctx, y, c = where_am_i()
    x, z = lax.div(dp, NZ), lax.rem(dp, NZ)
    partner = (dp, 2 * y + 1 - c)
    ahead = (dp, lax.rem(y + 1, NY) * 2 + c)
    behind = (dp, lax.rem(y + NY - 1, NY) * 2 + c)
    xdev = [(lax.rem(x + d, NX) * NZ + z, ctx) for d in range(NX)]
    zdev = [(x * NZ + lax.rem(z + d, NZ), ctx) for d in range(NZ)]
    tdev = [(dp, lax.rem(ctx + d, 2 * NY)) for d in range(2 * NY)]
    barrier, count = greet([xdev[1], xdev[3]] + zdev[1:] + tdev[1:])
    pl.semaphore_wait(barrier, count)
    r_eff, r_end, limit = marks[0], marks[1], marks[2]
    first = c == 0
    part_rows = ROWS_W // 2

    def w_rows(back, sub):
        owner = lax.rem(y + NY - back, NY) * 2 + c
        return pl.ds(pl.multiple_of(owner * ROWS_W + sub * part_rows, 16), part_rows)

    def w_copy(way, hop, sub):
        n = (way * 4 + hop - 1) * 2 + sub
        at = w_rows(hop - 1 if way == 0 else NY - hop + 1, sub)
        src = w_ref.at[sub * part_rows : (sub + 1) * part_rows] if hop == 1 else w_all.at[at]
        return rcopy(src, w_all.at[at], ws.at[n], wr.at[n], ahead if way == 0 else behind)

    def w_relay(way, hop, sub):
        n = (way * 4 + hop - 1) * 2 + sub
        at = w_rows(hop if way == 0 else NY - hop, sub)
        return rcopy(w_all.at[at], w_all.at[at], rs.at[n], rr.at[n], partner)

    messages = [(way, hop, sub) for hop in range(1, 5) for sub in range(2) for way in range(2) if hop < 4 or sub == way]
    copies = {m: w_copy(*m) for m in messages}
    relays = {m: w_relay(*m) for m in messages}
    for m in messages[:4]:
        copies[m].start()
    mine_w = pl.ds(pl.multiple_of(ctx * ROWS_W, 32), ROWS_W)
    own_relay = rcopy(w_ref, w_all.at[mine_w], rs.at[16], rr.at[16], partner)
    own_relay.start()
    local = pltpu.make_async_copy(w_ref, w_all.at[mine_w], lsem)
    local.start()

    pad = jnp.zeros((128 - H, CH), F32)
    row, col = iota((CH, CH), 0), iota((CH, CH), 1)
    scales = jnp.transpose(jnp.concatenate([scale_ref[...], jnp.zeros((128 - D // QB, CH), F32)], axis=0))

    def dequantize(n):
        for j in range(2 * n, 2 * n + 2):
            at = slice(j * QB, (j + 1) * QB)
            u_ref[:, at] = (codes_ref[:, at].astype(F32) * scales[:, j : j + 1]).astype(BF16)
            u_t[at, :] = jnp.transpose(u_ref[:, at])

    def decays():
        same = jnp.where(row >= r_eff, 1, 0) == jnp.where(col >= r_eff, 1, 0)
        bound[...] = jnp.where((col <= row) & same, 0.0, -1e30)
        upto = jnp.where(row <= col, 1.0, 0.0)
        keep_p = jnp.concatenate([keep_ref[...], pad], axis=0)
        cum_p = dot(keep_p, upto, precision=EXACT)
        cumr[...] = cum_p[:H]
        cum = jnp.transpose(cum_p)
        cum_t[...] = cum
        dts = jnp.transpose(jnp.concatenate([dt_ref[...], pad], axis=0))
        tcol = iota((CH, 128), 0)
        ds = jnp.where(tcol < limit, jnp.exp(cum), 0.0)
        de = jnp.where(tcol >= r_end, jnp.exp(cum[CH - 1 : CH, :] - cum), 0.0)
        ds_t[...] = ds
        de_t[...] = de
        dt_t[...] = dts
        carry = jnp.where(CH - 1 < limit, jnp.exp(cum_p[:H, CH - 1 : CH]), 0.0)
        c_own[...] = jnp.broadcast_to(carry, (H, 128))
        ssum[...] = jnp.zeros_like(ssum)
        racc[...] = jnp.zeros_like(racc)

    def weigh(g):
        at = slice(g * BLK, (g + 1) * BLK)
        head = lax.rem(iota((CH, BLK), 0), 128)
        spread = jnp.where(head == 8 * g + lax.div(iota((CH, BLK), 1), P_SIZE), 1.0, 0.0).astype(BF16)
        ds_hl = jnp.concatenate(split(ds_t[...]), axis=1)
        ws_hl = jnp.concatenate(split(de_t[...] * dt_t[...]), axis=1)
        dyb = split(dy_ref[:, at].astype(F32) * dot(ds_hl, spread))
        xb = split(x_ref[:, at].astype(F32) * dot(ws_hl, spread))
        for n in range(2):
            dyw[n, :, at] = dyb[n]
            xw[n, :, at] = xb[n]

    work = [functools.partial(dequantize, n) for n in range(10)]
    work += [decays] + [functools.partial(weigh, g) for g in range(5)]
    for n, m in enumerate(messages):
        if n % 2 == 0:
            for _ in range(2):
                if work:
                    work.pop(0)()
        way, hop, sub = m
        copies[m].wait_recv()
        onward = (way, hop + 1, sub)
        if onward in copies:
            copies[onward].start()
        relays[m].start()
    while work:
        work.pop(0)()
    local.wait()
    own_relay.wait_recv()
    for m in messages:
        relays[m].wait_recv()
    proj = dot(u_ref[...], w_all[...]).astype(BF16)
    b_mat, c_mat = proj[:, :N], proj[:, N:]

    mine = pl.multiple_of(c * HALF, 128)
    other_half = pl.multiple_of((1 - c) * HALF, 128)
    theirs = pl.ds(other_half, HALF)

    def local_states(base):
        def step(g, _):
            at = pl.ds(pl.multiple_of(base + g * 256, 128), 256)
            sloc[at, :] = dot2((xw[0, :, at], xw[1, :, at]), b_mat, TN)
            gloc[at, :] = dot2((dyw[0, :, at], dyw[1, :, at]), c_mat, TN)
            return 0

        lax.fori_loop(0, HALF // 256, step, 0)

    local_states(other_half)
    swap = [
        rcopy(c_own, c_prt, ps.at[0], pr.at[0], partner),
        rcopy(sloc.at[theirs], prt_s, ps.at[1], pr.at[1], partner),
        rcopy(gloc.at[theirs], prt_g, ps.at[2], pr.at[2], partner),
    ]
    for one in swap:
        one.start()
    local_states(mine)
    cross[...] = dot(c_mat, b_mat, NT)
    lane = iota((CH, 128), 1)

    @pl.when(y == 0)
    def _():
        frecv[...] = jnp.zeros_like(frecv)

    @pl.when(y == NY - 1)
    def _():
        vrecv[...] = jnp.zeros_like(vrecv)


    def chunk_rows(i):
        return pl.ds(pl.multiple_of(i * CHUNK, CHUNK), CHUNK)

    def decay(ref, i):
        h = c * (H // 2) + 2 * i
        return jnp.concatenate(
            [jnp.broadcast_to(ref[pl.ds(h + j, 1), :], (P_SIZE, N)) for j in range(2)], axis=0
        )

    def pick(i, own, other):
        a = own[pl.ds(pl.multiple_of(mine + i * CHUNK, CHUNK), CHUNK), :]
        b = other[chunk_rows(i), :]
        return jnp.where(first, a, b), jnp.where(first, b, a)

    def f_copy(i):
        return rcopy(fsend.at[chunk_rows(i)], frecv.at[chunk_rows(i)], fs.at[i], fr.at[i], ahead)

    def v_copy(i):
        return rcopy(vsend.at[chunk_rows(i)], vrecv.at[chunk_rows(i)], vs.at[i], vr.at[i], behind)

    def full_rows(i):
        return pl.ds(pl.multiple_of(mine + i * CHUNK, CHUNK), CHUNK)

    def s_copy(i):
        return rcopy(os.at[chunk_rows(i)], s_all.at[full_rows(i)], oss.at[i], osr.at[i], partner)

    def g_copy(i):
        return rcopy(og.at[chunk_rows(i)], g_all.at[full_rows(i)], ogs.at[i], ogr.at[i], partner)

    def slot(k, _):
        @pl.when(k < H // 2)
        def _():
            at = pl.ds(pl.multiple_of(k * 128, 128), 128)
            x2, dy2 = x_ref[:, at], dy_ref[:, at]
            turned = pltpu.roll(cum_t[...], lax.rem(128 - 2 * k, 128), 1)
            for j in range(2):
                h = 2 * k + j
                xm = jnp.where((lane < P_SIZE) if j == 0 else (lane >= P_SIZE), x2, jnp.zeros_like(x2))
                dots = dot(dy2, xm, NT)
                diff = turned[:, j : j + 1] - cumr[pl.ds(h, 1), :]
                mixed = jnp.exp(jnp.minimum(diff, bound[...])) * dots
                pair = mixed * cross[...]
                steps = dt_ref[pl.ds(h, 1), :]
                ssum[...] += mixed * steps
                cacc[pl.ds(h, 1), :] = jnp.sum(pair, axis=0, keepdims=True)
                rsum = jnp.sum(pair * steps, axis=1, keepdims=True)
                racc[...] += jnp.where(lane == h, rsum, 0.0)

        @pl.when(k == 0)
        def _():
            for one in swap:
                one.wait_recv()

        i = k - SKEW * y

        @pl.when((i >= 0) & (i < NCHUNK))
        def _():
            @pl.when(y > 0)
            def _():
                f_copy(i).wait_recv()

            a0, a1 = decay(c_own, i), decay(c_prt, i)
            a0, a1 = jnp.where(first, a0, a1), jnp.where(first, a1, a0)
            s0, s1 = pick(i, sloc, prt_s)
            state = frecv[chunk_rows(i), :].astype(F32)
            mid = a0 * state + s0

            @pl.when(y < NY - 1)
            def _():
                fsend[chunk_rows(i), :] = (a1 * mid + s1).astype(BF16)
                f_copy(i).start()

            os[chunk_rows(i), :] = jnp.where(first, mid, state)
            s_copy(i).start()
            s_all[full_rows(i), :] = jnp.where(first, state, mid)

        q = k - SKEW * (NY - 1 - y)

        @pl.when((q >= 0) & (q < NCHUNK))
        def _():
            @pl.when(y < NY - 1)
            def _():
                v_copy(q).wait_recv()

            a0, a1 = decay(c_own, q), decay(c_prt, q)
            a0, a1 = jnp.where(first, a0, a1), jnp.where(first, a1, a0)
            g0, g1 = pick(q, gloc, prt_g)
            state = vrecv[chunk_rows(q), :].astype(F32)
            mid = a1 * state + g1

            @pl.when(y > 0)
            def _():
                vsend[chunk_rows(q), :] = (a0 * mid + g0).astype(BF16)
                v_copy(q).start()

            og[chunk_rows(q), :] = jnp.where(first, state, mid)
            g_copy(q).start()
            g_all[full_rows(q), :] = jnp.where(first, mid, state)

        return 0

    lax.fori_loop(0, SLOTS, slot, 0)

    def drain(i, _):
        s_copy(i).wait()
        g_copy(i).wait()

        @pl.when(y < NY - 1)
        def _():
            f_copy(i).wait_send()

        @pl.when(y > 0)
        def _():
            v_copy(i).wait_send()

        return 0

    lax.fori_loop(0, NCHUNK, drain, 0)

    def outer(g, sums):
        x_t, e_t, gc, gb_, const = sums
        at = pl.ds(pl.multiple_of(g * BLK, BLK), BLK)
        s_blk, g_blk = s_all[at, :], g_all[at, :]
        gather = jnp.where(8 * g + lax.div(iota((BLK, 128), 0), P_SIZE) == iota((BLK, 128), 1), 1.0, 0.0).astype(BF16)
        fold = jnp.where(8 * g + lax.div(iota((128, BLK), 1), P_SIZE) == iota((128, BLK), 0), 1.0, 0.0).astype(BF16)
        both = split(s_blk * g_blk)
        s_blk, g_blk = split(s_blk), split(g_blk)
        inner_y = dot(c_mat, s_blk[0], NT) + dot(c_mat, s_blk[1], NT)
        inner_x = dot(b_mat, g_blk[0], NT) + dot(b_mat, g_blk[1], NT)
        prod_y = split(dy_ref[:, at].astype(F32) * inner_y)
        prod_x = split(x_ref[:, at].astype(F32) * inner_x)
        return (
            x_t + dot2(prod_y, gather),
            e_t + dot2(prod_x, gather),
            gc + dot2((dyw[0, :, at], dyw[1, :, at]), s_blk[0]) + dot(dyw[0, :, at], s_blk[1]),
            gb_ + dot2((xw[0, :, at], xw[1, :, at]), g_blk[0]) + dot(xw[0, :, at], g_blk[1]),
            const + dot(fold, both[0]) + dot(fold, both[1]),
        )

    sums = split(ssum[...])
    zero = jnp.zeros((CH, 128), F32)
    start = (zero, zero, dot2(sums, b_mat), dot2(sums, c_mat, TN), jnp.zeros((128, 128), F32))
    x_t, e_t, gc, gb_, const = lax.fori_loop(0, H * P_SIZE // BLK, outer, start)

    d_b, d_c = gb_.astype(BF16), gc.astype(BF16)
    d_own = jnp.where(first, d_b, d_c)
    d_oth = jnp.where(first, d_c, d_b)
    span = D // NX
    piece = span // NZ
    half = span // 2
    order = (2, 1, 3, 0)

    def u_rows(d):
        return u_t[pl.ds(pl.multiple_of(lax.rem(x + d, NX) * span, 128), span), :]

    pc = {}
    for d in order:
        psend[d] = dot(u_rows(d), d_oth)
        pc[d] = rcopy(psend.at[d], precv.at[d], qs.at[d], qr.at[d], partner)
        pc[d].start()
    xc = {}

    def x_send(n, value, d):
        xsend[n] = value.astype(BF16)
        xc[n] = rcopy(xsend.at[n], xrecv.at[n], xs_.at[n], xr.at[n], xdev[d])
        xc[n].start()

    for d in order:
        part = dot(u_rows(d), d_own)
        pc[d].wait_recv()
        own[d] = part + precv[d]
        if d == 2:
            x_send(0, own[2, :half], 1)
            x_send(1, own[2, half:], 3)
        if d == 1:
            x_send(2, own[1, half:], 1)
        if d == 3:
            x_send(3, own[3, :half], 3)
    xc[0].wait_recv()
    x_send(4, own[1, :half] + xrecv[0].astype(F32), 1)
    xc[1].wait_recv()
    x_send(5, own[3, half:] + xrecv[1].astype(F32), 3)

    ext_t = e_t * de_t[...]
    ext = jnp.transpose(ext_t)[:H]
    zed = jnp.transpose(ext_t * dt_t[...])[:H]
    late = jnp.transpose(x_t * ds_t[...] + racc[...])[:H]
    gdt_ref[...] = cacc[...] + ext
    since = jnp.where(row >= col, 1.0, 0.0)
    before = jnp.where(row < col, 1.0, 0.0)
    fixed = jnp.sum(const, axis=1, keepdims=True)[:H] * c_own[:, :1]
    gkeep_ref[...] = (
        dot(late - cacc[...] * dt_ref[...], since, precision=EXACT) + dot(zed, before, precision=EXACT) + fixed
    )

    for n in range(2, 6):
        xc[n].wait_recv()
    zsum[:half] = own[0, :half] + xrecv[4].astype(F32) + xrecv[3].astype(F32)
    zsum[half:] = own[0, half:] + xrecv[2].astype(F32) + xrecv[5].astype(F32)
    zc = {}
    for d in (4, 3, 5, 2, 6, 1, 7):
        at = pl.ds(pl.multiple_of(lax.rem(z + d, NZ) * piece, 16), piece)
        zsend[d] = zsum[at, :].astype(BF16)
        zc[d] = rcopy(zsend.at[d], zrecv.at[d], zs.at[d], zr.at[d], zdev[d])
        zc[d].start()
    total = zsum[pl.ds(pl.multiple_of(z * piece, 16), piece), :]
    for d in (1, 7, 2, 6, 3, 5, 4):
        zc[d].wait_recv()
        total = total + zrecv[d].astype(F32)
    tsend[...] = jnp.zeros_like(tsend)
    for i in range(2 * NY):
        tsend[i, 0:5, :] = total[5 * i : 5 * i + 5, :]
    tc = {}
    for d in range(1, 2 * NY):
        tc[d] = rcopy(
            tsend.at[lax.rem(ctx + d, 2 * NY)], trecv.at[d], ts.at[d], tr.at[d], tdev[d]
        )
        tc[d].start()
    same_core = tsend[ctx]
    other_core = jnp.zeros((8, N), F32)
    for d in range(1, 2 * NY):
        tc[d].wait_recv()
        if d % 2 == 0:
            same_core = same_core + trecv[d]
        else:
            other_core = other_core + trecv[d]
    grad_ref[:, :N] = jnp.where(first, same_core, other_core)[:5]
    grad_ref[:, N:] = jnp.where(first, other_core, same_core)[:5]
    for group in (copies, relays, pc, xc, zc, tc):
        for one in group.values():
            one.wait_send()
    own_relay.wait_send()
    for one in swap:
        one.wait_send()


VMEM = pl.BlockSpec(memory_space=pltpu.VMEM)
DMA = pltpu.SemaphoreType.DMA


def body(u_codes, u_scale, w_bc, xs, dt, log_keep, dy, lengths):
    v = pltpu.VMEM
    offset = lax.axis_index("ctx") * CH
    at = lengths[0, 0] - offset
    r_eff = jnp.where(at < 0, 1 << 20, at)
    r_end = jnp.where(r_eff < CH, r_eff, 0)
    limit = jnp.where(offset > 0, r_eff, 0)
    marks = jnp.stack([r_eff, r_end, limit]).astype(jnp.int32)
    hp = H * P_SIZE
    span = D // NX
    grad, gdt, gkeep = pl.pallas_call(
        mixer_kernel,
        out_shape=(
            jax.ShapeDtypeStruct((5, 2 * N), F32),
            jax.ShapeDtypeStruct((H, CH), F32),
            jax.ShapeDtypeStruct((H, CH), F32),
        ),
        in_specs=[pl.BlockSpec(memory_space=pltpu.SMEM)] + [VMEM] * 7,
        out_specs=(VMEM,) * 3,
        scratch_shapes=[
            v((D, CH), BF16), v((D, 2 * N), BF16), v((CH, D), BF16),
            v((2, CH, hp), BF16), v((2, CH, hp), BF16), v((hp, N), F32), v((hp, N), F32),
            v((HALF, N), F32), v((HALF, N), F32),
            v((H, 128), F32), v((H, 128), F32),
            v((HALF, N), BF16), v((HALF, N), BF16), v((HALF, N), BF16), v((HALF, N), BF16),
            v((hp, N), F32), v((hp, N), F32), v((HALF, N), F32), v((HALF, N), F32),
            v((CH, 128), F32), v((H, CH), F32), v((CH, CH), F32), v((CH, CH), F32), v((CH, CH), F32),
            v((H, CH), F32), v((CH, 128), F32), v((CH, 128), F32), v((CH, 128), F32), v((CH, 128), F32),
            v((NX, span, N), F32), v((NX, span, N), F32), v((NX, span, N), F32),
            v((6, span // 2, N), BF16), v((6, span // 2, N), BF16), v((span, N), F32),
            v((NZ, span // NZ, N), BF16), v((NZ, span // NZ, N), BF16),
            v((2 * NY, 8, N), F32), v((2 * NY, 8, N), F32),
            DMA((16,)), DMA((16,)), DMA((17,)), DMA((17,)), DMA,
            DMA((3,)), DMA((3,)),
        ] + [DMA((NCHUNK,))] * 8 + [
            DMA((NX,)), DMA((NX,)), DMA((6,)), DMA((6,)), DMA((NZ,)), DMA((NZ,)),
            DMA((2 * NY,)), DMA((2 * NY,)),
        ],
        compiler_params=pltpu.CompilerParams(
            collective_id=0, has_side_effects=True, vmem_limit_bytes=60 * 1024 * 1024
        ),
        name="mixer",
    )(marks, u_codes[0], u_scale[0].T, w_bc, xs[0], dy[0], dt[0], log_keep[0])
    return grad, gdt[None], gkeep[None]


def solution(mesh):
    placed = (
        P("dp", "ctx", None),
        P("dp", "ctx", None),
        P("ctx", None),
        P("dp", "ctx", None),
        P("dp", None, "ctx"),
        P("dp", None, "ctx"),
        P("dp", "ctx", None),
        P("dp", None),
    )
    return jax.shard_map(
        body,
        mesh=mesh,
        in_specs=placed,
        out_specs=(P(("dp", "ctx"), None), P("dp", None, "ctx"), P("dp", None, "ctx")),
        check_vma=False,
    )
```

time: 123 us -> 105 us (0.85)
  Pallas kernels: 117 us -> 97.3 us
  local copies, waits for them, and re-layouts: 4.02 us -> 5.43 us
    pallas_call x3 -> x1, Pallas kernels: 117 us -> 97.3 us  [body(): pl.pallas_call(mixer_kernel, out_shape=(jax.ShapeDtypeStruct((5, 2 * N),...]
    unnamed x8 -> x4, local copies, waits for them, and re-layouts: 4.02 us -> 5.43 us
where the time goes in v2:
time: 105 us
  Pallas kernels  97.3 us (93%)
  local copies, waits for them, and re-layouts  5.43 us (5%)
  between operations  1.3 us (1%)
    pallas_call x1, Pallas kernels, body(): pl.pallas_call(mixer_kernel, out_shape=(jax.ShapeDtypeStruct((5, 2 * N),...  97.3 us
    unnamed x4, local copies, waits for them, and re-layouts  5.43 us

profile of v2, /device:TPU:1, one launch (start us, length us, event | category | flops | bytes accessed | tf_op | source)
XLA Modules:
  0.0 104.6 jit_solution(7397069010288029199)
XLA Ops:
  1.3 0.6 pad_add_fusion.marks
  1.9 1.3 %copy.13 = f32[1,256,20]{1,2,0:T(8,128)} copy(f32[1,256,20]{1,0,2:T(1,128)} %param.9) | data formatting | bytes 40960
  3.2 97.3 %mixer.1 = (f32[5,256]{1,0:T(8,128)}, f32[40,256]{1,0:T(8,128)}, f32[40,256]{1,0:T(8,128)}) custom-call(s32[3]{0:T(128)} %pad_add_fusion.marks, bf16[256,2560]{1,0:T(8,128)(2,1)} %bitcast.17, f32[20,256]{1,0:T(8,128)} %bitcast.20, bf16[160,256]{1,0:T(8,128)(2,1)} %w_ref.1, bf16[256,2560]{1,0:T(8,128)(2,1)} %bitcast.18, bf16[256,2560]{1,0:T(8,128)(2,1)} %bitcast.19, ...), custom_call_target="tpu_custom_call" | custom-call | tf_op jit(solution)/shard_map/mixer/pallas_call | solution.py:472
  100.5 1.3 %copy.17 = f32[5,256]{1,0:T(8,128)} copy(f32[5,256]{1,0:T(8,128)} %get-tuple-element.12) | data formatting | bytes 10240
  101.8 1.4 %copy.18 = f32[1,40,256]{2,1,0:T(8,128)} copy(f32[1,40,256]{2,1,0:T(8,128)} %bitcast.24) | data formatting | bytes 81920
  103.2 1.4 %copy.19 = f32[1,40,256]{2,1,0:T(8,128)} copy(f32[1,40,256]{2,1,0:T(8,128)} %bitcast.23) | data formatting | bytes 81920

commit v3 on v2

--- a/solution.py
+++ b/solution.py
@@ -20,7 +20,7 @@
 ROWS_W = 160
 CHUNK = 128
 NCHUNK = HALF // CHUNK
-SKEW = 4
+SKEW = 6
 SLOTS = max(NCHUNK + SKEW * (NY - 1), H // 2)
 BLK = 512
 F32 = jnp.float32
@@ -364,8 +364,7 @@
     x_t, e_t, gc, gb_, const = lax.fori_loop(0, H * P_SIZE // BLK, outer, start)
 
     d_b, d_c = gb_.astype(BF16), gc.astype(BF16)
-    d_own = jnp.where(first, d_b, d_c)
-    d_oth = jnp.where(first, d_c, d_b)
+    d_both = jnp.concatenate([jnp.where(first, d_c, d_b), jnp.where(first, d_b, d_c)], axis=1)
     span = D // NX
     piece = span // NZ
     half = span // 2
@@ -376,7 +375,9 @@
 
     pc = {}
     for d in order:
-        psend[d] = dot(u_rows(d), d_oth)
+        product = dot(u_rows(d), d_both)
+        psend[d] = product[:, :N]
+        own[d] = product[:, N:]
         pc[d] = rcopy(psend.at[d], precv.at[d], qs.at[d], qr.at[d], partner)
         pc[d].start()
     xc = {}
@@ -387,9 +388,8 @@
         xc[n].start()
 
     for d in order:
-        part = dot(u_rows(d), d_own)
         pc[d].wait_recv()
-        own[d] = part + precv[d]
+        own[d] += precv[d]
         if d == 2:
             x_send(0, own[2, :half], 1)
             x_send(1, own[2, half:], 3)

time: 105 us -> 103 us (0.981)
  Pallas kernels: 97.3 us -> 95.6 us
    pallas_call x1, Pallas kernels: 97.3 us -> 95.6 us  [body(): pl.pallas_call(mixer_kernel, out_shape=(jax.ShapeDtypeStruct((5, 2 * N),...]
where the time goes in v3:
time: 103 us
  Pallas kernels  95.6 us (93%)
  local copies, waits for them, and re-layouts  5.43 us (5%)
  between operations  1.3 us (1%)
    pallas_call x1, Pallas kernels, body(): pl.pallas_call(mixer_kernel, out_shape=(jax.ShapeDtypeStruct((5, 2 * N),...  95.6 us
    unnamed x4, local copies, waits for them, and re-layouts  5.43 us

profile of v3, /device:TPU:1, one launch (start us, length us, event | category | flops | bytes accessed | tf_op | source)
XLA Modules:
  0.0 102.9 jit_solution(5568825428736440891)
XLA Ops:
  1.3 0.6 pad_add_fusion.marks
  1.9 1.3 %copy.13 = f32[1,256,20]{1,2,0:T(8,128)} copy(f32[1,256,20]{1,0,2:T(1,128)} %param.9) | data formatting | bytes 40960
  3.2 95.6 %mixer.1 = (f32[5,256]{1,0:T(8,128)}, f32[40,256]{1,0:T(8,128)}, f32[40,256]{1,0:T(8,128)}) custom-call(s32[3]{0:T(128)} %pad_add_fusion.marks, bf16[256,2560]{1,0:T(8,128)(2,1)} %bitcast.17, f32[20,256]{1,0:T(8,128)} %bitcast.20, bf16[160,256]{1,0:T(8,128)(2,1)} %w_ref.1, bf16[256,2560]{1,0:T(8,128)(2,1)} %bitcast.18, bf16[256,2560]{1,0:T(8,128)(2,1)} %bitcast.19, ...), custom_call_target="tpu_custom_call" | custom-call | tf_op jit(solution)/shard_map/mixer/pallas_call | solution.py:472
  98.8 1.3 %copy.17 = f32[5,256]{1,0:T(8,128)} copy(f32[5,256]{1,0:T(8,128)} %get-tuple-element.12) | data formatting | bytes 10240
  100.1 1.4 %copy.18 = f32[1,40,256]{2,1,0:T(8,128)} copy(f32[1,40,256]{2,1,0:T(8,128)} %bitcast.24) | data formatting | bytes 81920
  101.5 1.4 %copy.19 = f32[1,40,256]{2,1,0:T(8,128)} copy(f32[1,40,256]{2,1,0:T(8,128)} %bitcast.23) | data formatting | bytes 81920
